TPU v7x, 256 devices: a whole 4x4x8 slice. The times are simulated.
256 devices in a mesh: seq: 32 (over y, x, core), head: 8 (over z).
Axes of the slice: x: 4, y: 4, z: 8, core: 2. Of those that a mesh axis runs over, the one named last changes fastest.
Arguments:
- tokens: bfloat16 [32768, 2048], P(('seq', 'head')), may hold values from -6 to 6
- w_qkv: bfloat16 [2048, 3, 2048], P(None, None, 'head'), may hold values from -0.125 to 0.125
- w_beta: bfloat16 [2048, 16], P(None, 'head'), may hold values from -0.125 to 0.125
- beta_bias: float32 [16], P('head'), may hold values from -8 to 2
- w_out: bfloat16 [2048, 2048], P('head'), may hold values from -0.125 to 0.125
Outputs:
- mixed: bfloat16 [32768, 2048], P(('seq', 'head'))
All inputs are finite; a program needn't handle non-finite values.
Results may differ from a plain program's by a relative error of at most 0.015.
Values may be sent and summed in bfloat16 or wider, within the bound.
A program may use at most 64 MiB of HBM per device.

v0:
```python
import jax
import jax.numpy as jnp
from jax import lax
from jax.sharding import PartitionSpec as P

C = 64


epsilon = 1e-06


def unit_norm(values):
    return values * lax.rsqrt(jnp.sum(values * values, -1, keepdims=True) + epsilon)


def prepare(queries, key_rows, value_rows, strength):
    highest = lax.Precision.HIGHEST
    size_k = key_rows.shape[-1]
    similar = jnp.einsum("...id,...jd->...ij", key_rows, key_rows, precision=highest)
    system = jnp.eye(C, dtype=jnp.float32) + jnp.tril(similar * strength[..., :, None], -1)
    weighted = jnp.concatenate(
        [strength[..., None] * key_rows, strength[..., None] * value_rows], -1
    )
    solved = jax.scipy.linalg.solve_triangular(system, weighted, lower=True, unit_diagonal=True)
    w_fac = solved[..., :size_k]
    u_fac = solved[..., size_k:]
    masked = jnp.tril(jnp.einsum("...id,...jd->...ij", queries, key_rows, precision=highest))
    q_eff = queries - jnp.einsum("...ij,...jd->...id", masked, w_fac, precision=highest)
    return (w_fac, u_fac, masked, q_eff)


def body(tokens, w_qkv, w_beta, beta_bias, w_out):
    highest = lax.Precision.HIGHEST
    float_tokens = tokens.astype(jnp.float32)
    normed = (
        float_tokens * lax.rsqrt(jnp.mean(float_tokens * float_tokens, -1, keepdims=True) + epsilon)
    ).astype(jnp.bfloat16)
    gathered = lax.all_gather(normed, "head", axis=0, tiled=True)
    length = gathered.shape[0]
    model_width = gathered.shape[1]
    local_heads = beta_bias.shape[0]
    size_k = w_out.shape[0] // local_heads
    projected = jnp.dot(
        gathered, w_qkv.reshape(model_width, -1), preferred_element_type=jnp.float32
    )
    projected = projected.reshape(length, 3, local_heads, size_k)
    queries = unit_norm(jax.nn.silu(projected[:, 0]))
    key_rows = unit_norm(jax.nn.silu(projected[:, 1]))
    value_rows = jax.nn.silu(projected[:, 2])
    strength = jax.nn.sigmoid(
        jnp.dot(gathered, w_beta, preferred_element_type=jnp.float32) + beta_bias
    )
    block_count = length // C

    def blocks(values):
        return values.reshape(block_count, C, local_heads, -1).transpose(0, 2, 1, 3)

    key_blocks = blocks(key_rows)
    w_fac, u_fac, masked, q_eff = prepare(
        blocks(queries),
        key_blocks,
        blocks(value_rows),
        strength.reshape(block_count, C, local_heads).transpose(0, 2, 1),
    )
    identity = jnp.broadcast_to(jnp.eye(size_k, dtype=jnp.float32), (local_heads, size_k, size_k))
    empty_state = jnp.zeros((local_heads, size_k, size_k), jnp.float32)

    def advance(pair_state, pieces):
        transition, state = pair_state
        w_blk, u_blk, m_blk, qe_blk, k_blk = pieces
        local_out = jnp.einsum("hcj,hvj->hcv", qe_blk, state, precision=highest) + jnp.einsum(
            "hcd,hdv->hcv", m_blk, u_blk, precision=highest
        )
        fold_query = jnp.einsum("hcj,hij->hci", qe_blk, transition, precision=highest)
        trans_w = jnp.einsum("hij,hcj->hic", transition, w_blk, precision=highest)
        new_transition = transition - jnp.einsum("hic,hcd->hid", trans_w, k_blk, precision=highest)
        state_w = jnp.einsum("hvj,hcj->hvc", state, w_blk, precision=highest)
        change = u_blk.transpose(0, 2, 1) - state_w
        new_state = state + jnp.einsum("hvc,hcd->hvd", change, k_blk, precision=highest)
        return ((new_transition, new_state), (local_out, fold_query))

    (trans_end, state_end), (local_all, fold_all) = lax.scan(
        advance, (identity, empty_state), (w_fac, u_fac, masked, q_eff, key_blocks)
    )
    all_trans, all_state = (
        lax.all_gather(trans_end[None].astype(jnp.bfloat16), "seq", axis=0, tiled=True).astype(
            jnp.float32
        ),
        lax.all_gather(state_end[None].astype(jnp.bfloat16), "seq", axis=0, tiled=True).astype(
            jnp.float32
        ),
    )
    own_index = lax.axis_index("seq")

    def chain_step(state, pieces):
        transition, partial_value, position = pieces
        advanced = jnp.einsum("hvj,hjk->hvk", state, transition, precision=highest) + partial_value
        return (jnp.where(position < own_index, advanced, state), None)

    incoming, _ = lax.scan(
        chain_step,
        empty_state,
        (all_trans, all_state, jnp.arange(all_trans.shape[0], dtype=jnp.int32)),
    )
    outputs = local_all + jnp.einsum("nhci,hvi->nhcv", fold_all, incoming, precision=highest)
    outputs = outputs.transpose(0, 2, 1, 3).reshape(length, local_heads, size_k)
    outputs = outputs * lax.rsqrt(jnp.mean(outputs * outputs, -1, keepdims=True) + epsilon)
    flat_out = outputs.reshape(length, local_heads * size_k).astype(jnp.bfloat16)
    return lax.psum_scatter(
        jnp.dot(flat_out, w_out, preferred_element_type=jnp.float32).astype(jnp.bfloat16),
        "head",
        scatter_dimension=0,
        tiled=True,
    )


def solution(mesh):
    return jax.shard_map(
        body,
        mesh=mesh,
        in_specs=(
            P(("seq", "head"), None),
            P(None, None, "head"),
            P(None, "head"),
            P("head"),
            P("head", None),
        ),
        out_specs=P(("seq", "head"), None),
        check_vma=False,
    )
```

profile of v0, /device:TPU:1, one launch (start us, length us, event | category | flops | bytes accessed | tf_op | source)
XLA Modules:
  0.0 669.9 jit_solution(6696784962300135828)
XLA Ops:
  7.9 2.0 fusion.63
  10.0 4.8 copy.39
  14.8 53.6 %all-gather.6.cloned.1.call-done = bf16[1024,2048]{1,0:T(8,128)(2,1)} async-done(((bf16[128,2048]{1,0:T(8,128)(2,1)}), bf16[1024,2048]{1,0:T(8,128)(2,1)}) %all-gather.6.cloned.1.call-update) | async-done | bytes 4194320 | tf_op jit(solution)/shard_map/all_gather | solution.py:38
  68.4 6.2 fusion.45
  75.3 1.7 fusion.85
  77.2 3.4 fusion.61
  80.7 2.7 broadcast_multiply_fusion
  83.4 2.7 fusion.57
  86.1 158.7 %custom-call.4 = f32[16,2,1,64,64]{3,4,2,1,0:T(8,128)} custom-call(f32[16,2,1,64,64]{4,3,2,1,0:T(8,128)} %fusion.57), custom_call_target="InvertDiagBlocksLowerTriangular" | custom-call | tf_op jit(solution)/shard_map/jit(_solve_triangular)/vmap(vmap())/triangular_solve | solution.py:24
  244.9 3.5 fusion.47
  249.7 2.0 convolution_select_fusion
  251.7 2.4 convolution_subtract_fusion.2
  254.2 127.7 %while.28 = (s32[]{:T(128)}, f32[2,128,128]{2,1,0:T(8,128)S(1)}, f32[2,128,128]{2,1,0:T(8,128)S(1)}, f32[16,2,64,128]{3,2,0,1:T(8,128)}, f32[16,2,64,128]{3,2,0,...) while((s32[]{:T(128)}, f32[2,128,128]{2,1,0:T(8,128)S(1)}, ...), condition=%wide.region_4.5_spmd.clone, body=%wide.region_3.4_spmd.clone.sunk | while | flops 163774464 | bytes 2167433 | solution.py:82
  258.8 1.8 fusion.138
  263.5 1.7 fusion.137
  266.8 1.8 fusion.138
  271.5 1.7 fusion.137
  274.8 1.8 fusion.138
  279.5 1.7 fusion.137
  282.8 1.8 fusion.138
  287.5 1.7 fusion.137
  290.8 1.8 fusion.138
  298.7 1.8 fusion.138
  303.4 1.7 fusion.137
  306.7 1.8 fusion.138
  311.3 1.7 fusion.137
  314.6 1.8 fusion.138
  322.6 1.8 fusion.138
  330.6 1.8 fusion.138
  335.3 1.7 fusion.137
  338.6 1.8 fusion.138
  343.2 1.7 fusion.137
  346.5 1.8 fusion.138
  354.5 1.8 fusion.138
  359.2 1.7 fusion.137
  362.5 1.8 fusion.138
  367.2 1.7 fusion.137
  370.5 1.8 fusion.138
  375.1 1.7 fusion.137
  378.4 1.8 fusion.138
  383.3 47.1 %all-gather.8.cloned.1.call-done = bf16[64,128,128]{2,1,0:T(8,128)(2,1)} async-done(((bf16[2,128,128]{2,1,0:T(8,128)(2,1)}), bf16[64,128,128]{2,1,0:T(8,128)(2,1)}) %all-gather.8.cloned.1.call-update) | async-done | bytes 2097168 | tf_op jit(solution)/shard_map/all_gather | solution.py:86
  430.4 4.1 convert.3
  434.5 46.5 %all-gather.10.cloned.1.call-done = bf16[64,128,128]{2,1,0:T(8,128)(2,1)} async-done(((bf16[2,128,128]{2,1,0:T(8,128)(2,1)}), bf16[64,128,128]{2,1,0:T(8,128)(2,1)}) %all-gather.10.cloned.1.call-update) | async-done | bytes 2097168 | tf_op jit(solution)/shard_map/all_gather | solution.py:89
  481.0 4.1 convert.4
  485.1 115.8 %while.29 = (s32[]{:T(128)}, f32[2,128,128]{1,2,0:T(8,128)S(1)}, s32[32]{0:T(128)S(1)}, s32[]{:T(128)}, f32[32,2,128,128]{3,2,1,0:T(8,128)}, /*index=5*/f32[32,2,128,128]{3,2,1,0:T(8,128)}, s32[]{:T(128)}, s32[]{:T(128)}) while((s32[]{:T(128)}, f32[2,128,128]{1,2,0:T(8,128)S(1)}, s32[32]{0:T(128)S(1)}, s32[]{:T(128)}, ...), condition=%wide.region_6.7_spmd.clone, body=%wide.region_5.6_spmd.clone.sunk | while | flops 50462724 | bytes 1443959 | solution.py:100
  600.9 2.4 multiply_reduce_fusion
  605.6 3.2 convolution_convert_fusion
  608.9 54.4 %reduce-scatter.2.cloned.1.call-done = bf16[128,2048]{1,0:T(8,128)(2,1)} async-done(((bf16[1024,2048]{1,0:T(8,128)(2,1)}), bf16[128,2048]{1,0:T(8,128)(2,1)}) %reduce-scatter.2.cloned.1.call-update) | async-done | bytes 524304 | tf_op jit(solution)/shard_map/reduce_scatter | solution.py:109
  (293 shorter events, 179.7 us)
Async XLA Ops:
  6.5 599.1 %copy-start = (bf16[256,2048]{1,0:T(8,128)(2,1)S(1)}, bf16[256,2048]{1,0:T(8,128)(2,1)}, u32[]{:S(2)}) copy-start(bf16[256,2048]{1,0:T(8,128)(2,1)} %param.13) | copy-start | bytes 3145732
  6.5 61.9 %all-gather.6.cloned.1.call-start = ((), (), s32[]{:S(2)}) async-start(), calls=%async_computation.1 | async-start | bytes 4718592 | tf_op jit(solution)/shard_map/all_gather | solution.py:38
  9.9 420.6 %all-gather.8.cloned.1.call-start = ((), (), s32[]{:S(2)}) async-start(), calls=%async_computation.3 | async-start | bytes 2162688 | tf_op jit(solution)/shard_map/all_gather | solution.py:86
  75.3 1.8 copy-start.4
  75.3 1.8 copy-start.5
  248.4 1.3 copy-start.2
  251.7 2.5 copy-start.3
  382.5 98.5 %all-gather.10.cloned.1.call-start = ((), (), s32[]{:S(2)}) async-start(), calls=%async_computation.4 | async-start | bytes 2162688 | tf_op jit(solution)/shard_map/all_gather | solution.py:89
  383.3 280.0 %reduce-scatter.2.cloned.1.call-start = ((), (), s32[]{:S(2)}) async-start(), calls=%async_computation.2 | async-start | bytes 4718592 | tf_op jit(solution)/shard_map/reduce_scatter | solution.py:109
  485.1 115.8 %copy-start.1 = (f32[16,2,64,128]{3,2,0,1:T(8,128)S(1)}, f32[16,2,64,128]{3,2,0,1:T(8,128)}, u32[]{:S(2)}) copy-start(f32[16,2,64,128]{3,2,0,1:T(8,128)} %get-tuple-element.92) | copy-start | bytes 3145732
Sparse Core Ops, SparseCore 0:
  10.0 58.3 all-gather.5
  382.7 47.7 all-gather.7
  433.0 47.9 all-gather.9
  609.0 54.2 reduce-scatter.1
where the time goes:
time: 675 us; the launch traced here: 670 us
  waiting for transfers between devices  202 us (30%)
  matrix products  194 us (29%)
  other arithmetic  175 us (26%)
  local copies, waits for them, and re-layouts  61.9 us (9%)
  loops' own time  23.5 us (3%)
  between operations  13.4 us (2%)
    another operation x4, other arithmetic, prepare(): jax.scipy.linalg.solve_triangular(system, weighted, lower=True, unit_diag...  159 us
    reduce_scatter x1, waiting for transfers between devices, body(): lax.psum_scatter(jnp.dot(flat_out, w_out, preferred_element_type=jnp.floa...  54.4 us
    all_gather x1, waiting for transfers between devices, body(): gathered = lax.all_gather(normed, 'head', axis=0, tiled=True)  53.6 us
    dynamic_slice x96, local copies, waits for them, and re-layouts, body(): lax.scan(chain_step, empty_state, (all_trans, all_state, jnp.arange(all_t...  51.2 us
    all_gather x1, waiting for transfers between devices, body(): lax.all_gather(trans_end[None].astype(jnp.bfloat16), 'seq', axis=0, tiled...  47.1 us
    all_gather x1, waiting for transfers between devices, body(): lax.all_gather(state_end[None].astype(jnp.bfloat16), 'seq', axis=0, tiled...  46.5 us
    dot_general x32, matrix products, chain_step(): jnp.einsum('hvj,hjk->hvk', state, transition, precision=highest)  41.8 us
    dot_general x16, matrix products, advance(): jnp.einsum('hcj,hij->hci', qe_blk, transition, precision=highest)  29.4 us
  transfers between devices with their start and end apart: 4, of which 4 were waited for; matrix products, arithmetic and copies ran while one was open for 1% of the time, Pallas kernels for 0%

commit v1 on v0

v1 whole, which is shorter than its diff:
```python
import jax
import jax.numpy as jnp
from jax import lax
from jax.experimental import pallas as pl
from jax.experimental.pallas import tpu as pltpu
from jax.sharding import PartitionSpec as P

F32 = jnp.float32
BF16 = jnp.bfloat16
MESH = pl.DeviceIdType.MESH
EPS = 1e-6
NZ = 8
NX = 4
NY = 4
NC = 2
C = 64
DK = 128
D = 2048

NN = (((1,), (0,)), ((), ()))
NT = (((1,), (1,)), ((), ()))
TN = (((0,), (0,)), ((), ()))


def halves(a):
    hi = a.astype(BF16)
    lo = (a - hi.astype(F32)).astype(BF16)
    return hi, lo


def dot3(a, b, dims=NN):
    ca = dims[0][0][0]
    cb = dims[0][1][0]
    ah, al = halves(a)
    bh, bl = halves(b)
    return lax.dot_general(
        jnp.concatenate([ah, al, ah], ca),
        jnp.concatenate([bh, bh, bl], cb),
        dims,
        preferred_element_type=F32,
    )


def compose(first, second):
    return first + dot3(first, second[:DK]) + second


def kernel(
    tok_ref,
    w3_hbm,
    wb_ref,
    bias_ref,
    wo_hbm,
    out_ref,
    g,
    w3,
    wbt,
    wo,
    qe,
    mu,
    db,
    tot,
    lv,
    xs,
    xr,
    sin,
    ss,
    osend,
    fbuf,
    acc,
    lsem,
    agr_s,
    agr_r,
    agl_s,
    agl_r,
    wz_s,
    wz_r,
    w1_s,
    w1_r,
    w2_s,
    w2_r,
    wc_s,
    wc_r,
    sc_s,
    sc_r,
    a2_s,
    a2_r,
):
    s = lax.axis_index("seq")
    z = lax.axis_index("head")
    c = lax.rem(s, NC)
    x = lax.rem(s // NC, NX)
    y = s // (NC * NX)

    def at_z(d):
        return (s, lax.rem(z + d, NZ))

    def at_x(d):
        return ((y * NX + lax.rem(x + d, NX)) * NC + c, z)

    def at_y(d):
        return ((lax.rem(y + d, NY) * NX + x) * NC + c, z)

    partner = ((y * NX + x) * NC + (1 - c), z)

    peers = [at_z(d) for d in range(1, NZ)]
    peers += [at_x(d) for d in range(1, NX)]
    peers += [at_y(d) for d in range(1, NY)]
    peers += [partner]
    barrier = pltpu.get_barrier_semaphore()
    for p in peers:
        pl.semaphore_signal(barrier, inc=1, device_id=p, device_id_type=MESH)

    cp_w3 = pltpu.make_async_copy(w3_hbm, w3, lsem.at[0])
    cp_w3.start()
    cp_wo = pltpu.make_async_copy(
        wo_hbm.at[y, x, :, pl.ds(pl.multiple_of(c * 1024, 1024), 1024)],
        wo.at[c, z, y, x],
        lsem.at[1],
    )
    cp_wo.start()

    for j in range(2):
        t = tok_ref[j * C : (j + 1) * C, :].astype(F32)
        ms = jnp.mean(t * t, -1, keepdims=True)
        g[z, j] = (t * lax.rsqrt(ms + EPS)).astype(BF16)

    pl.semaphore_wait(barrier, len(peers))

    def remote(src, dst, ssem, rsem, dev):
        return pltpu.make_async_remote_copy(
            src_ref=src, dst_ref=dst, send_sem=ssem, recv_sem=rsem,
            device_id=dev, device_id_type=MESH,
        )

    def right(i):
        o = lax.rem(z + NZ - i // 2, NZ)
        ref = g.at[o, lax.rem(i, 2)]
        return remote(ref, ref, agr_s.at[i], agr_r.at[i], at_z(1))

    def left(i):
        o = lax.rem(z + i // 2, NZ)
        ref = g.at[o, jnp.where(i == 6, 1, lax.rem(i, 2))]
        return remote(ref, ref, agl_s.at[i], agl_r.at[i], at_z(NZ - 1))

    for i in range(2):
        right(jnp.int32(i)).start()
        left(jnp.int32(i)).start()

    cp_wo.wait()

    def wz(d):
        ref = wo.at[c, z, y, x]
        return remote(ref, ref, wz_s.at[d - 1], wz_r.at[d - 1], at_z(d))

    def w1x(d):
        ref = wo.at[c, pl.ds(0, 4), y, x]
        return remote(ref, ref, w1_s.at[d - 1], w1_r.at[d - 1], at_x(d))

    def w1y(d):
        ref = wo.at[c, pl.ds(4, 4), y, x]
        return remote(ref, ref, w1_s.at[d + 2], w1_r.at[d + 2], at_y(d))

    def w2y(d):
        ref = wo.at[c, pl.ds(0, 4), y]
        return remote(ref, ref, w2_s.at[d - 1], w2_r.at[d - 1], at_y(d))

    def w2x(d):
        ref = wo.at[c, pl.ds(4, 4), :, x]
        return remote(ref, ref, w2_s.at[d + 2], w2_r.at[d + 2], at_x(d))

    for d in range(1, NZ):
        wz(d).start()

    for h in range(2):
        row = jnp.broadcast_to(wb_ref[h : h + 1, :].astype(F32), (DK, D))
        wbt[:, h * DK : (h + 1) * DK] = row.T.astype(BF16)
    cp_w3.wait()

    ri = lax.broadcasted_iota(jnp.int32, (DK, DK), 0)
    ci = lax.broadcasted_iota(jnp.int32, (DK, DK), 1)
    same = (ri // C) == (ci // C)
    strict = same & (ri > ci)
    lower = same & (ri >= ci)
    eye = jnp.where(ri == ci, 1.0, 0.0).astype(F32)

    def level_mask(b):
        return (
            ((ri // (2 * b)) == (ci // (2 * b)))
            & (lax.rem(ri // b, 2) == 1)
            & (lax.rem(ci // b, 2) == 0)
        )

    def unit(v):
        return v * lax.rsqrt(jnp.sum(v * v, -1, keepdims=True) + EPS)

    def silu(v):
        return v / (1.0 + jnp.exp(-v))

    def joint(pieces):
        rows = jnp.concatenate([g[o, j] for o, j in pieces], 0)
        proj = [
            jnp.dot(rows, w3[p], preferred_element_type=F32) for p in range(3)
        ]
        pre = jnp.dot(rows, wbt[...], preferred_element_type=F32)
        qs = silu(proj[0])
        ks = silu(proj[1])
        vs = silu(proj[2])
        qh = [unit(qs[:, h * DK : (h + 1) * DK]) for h in range(2)]
        kh = [unit(ks[:, h * DK : (h + 1) * DK]) for h in range(2)]
        vh = [vs[:, h * DK : (h + 1) * DK] for h in range(2)]
        bh = [
            1.0 / (1.0 + jnp.exp(-(pre[:, h * DK : (h + 1) * DK] + bias_ref[h])))
            for h in range(2)
        ]
        for a, (o, j) in enumerate(pieces):
            part = slice(a * C, (a + 1) * C)
            q = jnp.concatenate([qh[0][part], qh[1][part]], 0)
            k = jnp.concatenate([kh[0][part], kh[1][part]], 0)
            v = jnp.concatenate([vh[0][part], vh[1][part]], 0)
            b = jnp.concatenate([bh[0][part], bh[1][part]], 0)
            both = dot3(jnp.concatenate([k, q], 0), k, NT)
            low = jnp.where(strict, both[:DK] * b, 0.0)
            masked = jnp.where(lower, both[DK:], 0.0)
            inv = eye - jnp.where(level_mask(1), low, 0.0)
            for size in (2, 4, 8, 16, 32):
                part_low = jnp.where(level_mask(size), low, 0.0)
                inv = inv - dot3(dot3(inv, part_low), inv)
            wu = dot3(inv, jnp.concatenate([b * k, b * v], 1))
            mwu = dot3(masked, wu)
            blk = 2 * o + j
            for h in range(2):
                hp = slice(h * C, (h + 1) * C)
                qe[h, blk] = q[hp] - mwu[hp, :DK]
                mu[h, blk] = mwu[hp, DK:]
                pair = dot3(wu[hp], k[hp], TN)
                db[h, blk, :DK] = -pair[:DK]
                db[h, blk, DK:] = pair[DK:]

    def step(t, carry):
        i = t - 1

        @pl.when(t >= 1)
        def _():
            right(i).wait_recv()

            @pl.when(i <= 4)
            def _():
                right(i + 2).start()

            left(i).wait_recv()

            @pl.when(i <= 3)
            def _():
                left(i + 2).start()

            @pl.when(i == 5)
            def _():
                left(i + 1).start()

        @pl.when(t == 1)
        def _():
            for d in range(1, NZ):
                wz(d).wait_recv()
            for d in range(1, NX):
                w1x(d).start()
                w1y(d).start()

        @pl.when(t == 3)
        def _():
            for d in range(1, NX):
                w1x(d).wait_recv()
                w1y(d).wait_recv()
            for d in range(1, NX):
                w2y(d).start()
                w2x(d).start()

        hop = (i + 2) // 2
        mid = jnp.logical_and(t >= 1, t <= 6)
        hop = jnp.where(t == 0, 0, hop)
        ja = jnp.where(mid, lax.rem(t + 1, 2), 0)
        jb = jnp.where(mid, lax.rem(t + 1, 2), 1)
        oa = lax.rem(z + NZ - hop, NZ)
        ob = lax.rem(z + hop, NZ)
        joint([(oa, ja), (ob, jb)])
        return carry

    lax.fori_loop(0, 8, step, 0)

    for d in range(1, NX):
        w2y(d).wait_recv()
        w2x(d).wait_recv()

    def fold_in(b, carry):
        nxt = []
        for h in range(2):
            here = db[h, b]
            db[h, b] = carry[h]
            nxt.append(compose(carry[h], here))
        return tuple(nxt)

    zero = jnp.zeros((2 * DK, DK), F32)
    ends = lax.fori_loop(0, 2 * NZ, fold_in, (zero, zero))
    for h in range(2):
        tot[h] = ends[h]

    def core_swap():
        return remote(tot.at[1 - c], lv.at[c], sc_s.at[0], sc_r.at[0], partner)

    core_swap().start()
    lv[c] = tot[c]

    def fold_queries(first, last):
        def one(b, carry):
            for h in range(2):
                q = qe[h, b]
                both = dot3(q, db[h, b], NT)
                qe[h, b] = q + both[:, :DK]
                mu[h, b] = mu[h, b] + both[:, DK:]
            return carry

        lax.fori_loop(first, last, one, 0)

    core_swap().wait_recv()

    wc = remote(wo.at[c], wo.at[c], wc_s.at[0], wc_r.at[0], partner)
    wc.start()

    group = compose(lv[0], lv[1])
    before = jnp.zeros((2 * DK, DK), F32)
    xp = jnp.where(lax.rem(x, 2) == 0, 1, NX - 1)
    yp = jnp.where(lax.rem(y, 2) == 0, 1, NY - 1)
    xq = lax.rem(2 * NX - 1 - 2 * x, NX)
    yq = lax.rem(2 * NY - 1 - 2 * y, NY)
    levels = [
        (at_x(xp), lax.rem(x, 2) == 0),
        (at_x(xq), x < 2),
        (at_y(yp), lax.rem(y, 2) == 0),
        (at_y(yq), y < 2),
    ]
    sends = []
    for n, (dev, is_low) in enumerate(levels):
        xs[n] = group.astype(BF16)
        cp = remote(xs.at[n], xr.at[n], sc_s.at[n + 1], sc_r.at[n + 1], dev)
        cp.start()
        sends.append(cp)
        fold_queries(4 * n, 4 * n + 4)
        cp.wait_recv()
        other = xr[n].astype(F32)
        low = jnp.broadcast_to(is_low.astype(jnp.int32), (2 * DK, DK)) > 0
        if n < 3:
            group = compose(jnp.where(low, group, other), jnp.where(low, other, group))
        before = jnp.where(low, before, compose(other, before))

    s0 = before[DK:]
    first = lv[0]
    s1 = s0 + dot3(s0, first[:DK]) + first[DK:]
    zero_core = jnp.broadcast_to(c, (DK, DK)) == 0
    ss[...] = jnp.where(zero_core, s1, s0)
    give = remote(ss, sin.at[c], sc_s.at[5], sc_r.at[5], partner)
    give.start()
    sin[c] = jnp.where(zero_core, s0, s1)
    give.wait_recv()

    def a2a(d, o):
        return remote(osend.at[o], fbuf.at[z], a2_s.at[d - 1], a2_r.at[d - 1], (s, o))

    def emit(i, carry):
        d = jnp.where(lax.rem(i, 2) == 1, 4 - (i + 1) // 2, 4 + i // 2)
        o = lax.rem(z + d, NZ)
        cols = []
        for h in range(2):
            q = jnp.concatenate([qe[h, 2 * o], qe[h, 2 * o + 1]], 0)
            m = jnp.concatenate([mu[h, 2 * o], mu[h, 2 * o + 1]], 0)
            full = m + dot3(q, sin[h], NT)
            ms = jnp.mean(full * full, -1, keepdims=True)
            cols.append((full * lax.rsqrt(ms + EPS)).astype(BF16))
        rows = jnp.concatenate(cols, 1)

        @pl.when(i < 7)
        def _():
            osend[o] = rows
            a2a(d, o).start()

        @pl.when(i == 7)
        def _():
            fbuf[z] = rows

        return carry

    lax.fori_loop(0, NZ, emit, 0)

    wc.wait_recv()

    def finish(i, carry):
        d = jnp.where(lax.rem(i, 2) == 1, (i + 1) // 2, lax.rem(NZ - i // 2, NZ))
        src = lax.rem(z + NZ - d, NZ)

        @pl.when(i >= 1)
        def _():
            remote(
                osend.at[src], fbuf.at[src], a2_s.at[d - 1], a2_r.at[d - 1], (s, src)
            ).wait_recv()

        rows = fbuf[src]
        for half in range(2):
            w = wo[half, src].reshape(2 * DK, 1024)
            term = jnp.dot(rows, w, preferred_element_type=F32)
            cols = slice(half * 1024, (half + 1) * 1024)

            @pl.when(i == 0)
            def _():
                acc[:, cols] = term

            @pl.when(i >= 1)
            def _():
                acc[:, cols] = acc[:, cols] + term

        return carry

    lax.fori_loop(0, NZ, finish, 0)
    out_ref[...] = acc[...].astype(BF16)

    for i in range(7):
        right(jnp.int32(i)).wait_send()
        left(jnp.int32(i)).wait_send()
    for d in range(1, NZ):
        wz(d).wait_send()
        a2a(d, lax.rem(z + d, NZ)).wait_send()
    for d in range(1, NX):
        w1x(d).wait_send()
        w1y(d).wait_send()
        w2x(d).wait_send()
        w2y(d).wait_send()
    wc.wait_send()
    core_swap().wait_send()
    for cp in sends:
        cp.wait_send()
    give.wait_send()


def body(tokens, w_qkv, w_beta, beta_bias, w_out):
    w3 = jnp.transpose(w_qkv, (1, 0, 2))
    wb = jnp.transpose(w_beta, (1, 0))
    wo = w_out.reshape(NY, NX, 16, D)
    vmem = pl.BlockSpec(memory_space=pltpu.VMEM)
    hbm = pl.BlockSpec(memory_space=pl.ANY)
    smem = pl.BlockSpec(memory_space=pltpu.SMEM)
    dma = pltpu.SemaphoreType.DMA
    return pl.pallas_call(
        kernel,
        out_shape=jax.ShapeDtypeStruct((2 * C, D), BF16),
        in_specs=[vmem, hbm, vmem, smem, hbm],
        out_specs=vmem,
        scratch_shapes=[
            pltpu.VMEM((NZ, 2, C, D), BF16),
            pltpu.VMEM((3, D, 2 * DK), BF16),
            pltpu.VMEM((D, 2 * DK), BF16),
            pltpu.VMEM((2, NZ, NY, NX, 16, 1024), BF16),
            pltpu.VMEM((2, 16, C, DK), F32),
            pltpu.VMEM((2, 16, C, DK), F32),
            pltpu.VMEM((2, 16, 2 * DK, DK), F32),
            pltpu.VMEM((2, 2 * DK, DK), F32),
            pltpu.VMEM((2, 2 * DK, DK), F32),
            pltpu.VMEM((4, 2 * DK, DK), BF16),
            pltpu.VMEM((4, 2 * DK, DK), BF16),
            pltpu.VMEM((2, DK, DK), F32),
            pltpu.VMEM((DK, DK), F32),
            pltpu.VMEM((NZ, 2 * C, 2 * DK), BF16),
            pltpu.VMEM((NZ, 2 * C, 2 * DK), BF16),
            pltpu.VMEM((2 * C, D), F32),
            dma((2,)),
            dma((7,)),
            dma((7,)),
            dma((7,)),
            dma((7,)),
            dma((7,)),
            dma((7,)),
            dma((6,)),
            dma((6,)),
            dma((6,)),
            dma((6,)),
            dma((1,)),
            dma((1,)),
            dma((6,)),
            dma((6,)),
            dma((7,)),
            dma((7,)),
        ],
        compiler_params=pltpu.CompilerParams(
            collective_id=0, has_side_effects=True, vmem_limit_bytes=60 * 1024 * 1024
        ),
        name="delta_layer",
    )(tokens, w3, wb, beta_bias, wo)


def solution(mesh):
    return jax.shard_map(
        body,
        mesh=mesh,
        in_specs=(
            P(("seq", "head"), None),
            P(None, None, "head"),
            P(None, "head"),
            P("head"),
            P("head", None),
        ),
        out_specs=P(("seq", "head"), None),
        check_vma=False,
    )
```

time: 675 us -> 109 us (0.16)
  waiting for transfers between devices: 202 us -> 0 us
  matrix products: 194 us -> 0 us
  other arithmetic: 175 us -> 0 us
  Pallas kernels: 0 us -> 107 us
  local copies, waits for them, and re-layouts: 61.9 us -> 1.88 us
  loops' own time: 23.5 us -> 0 us
  between operations: 13.4 us -> 0.01 us
    dot_general x151 -> x0, matrix products: 191 us -> none  [the longest x32 41.8 us: chain_step(): jnp.einsum('hvj,hjk->hvk', state, transition, precision=highest)]
    another operation x6 -> x0, other arithmetic: 159 us -> none  [the longest x4 159 us: prepare(): jax.scipy.linalg.solve_triangular(system, weighted, lower=True, unit_diag...]
    all_gather x3 -> x0, waiting for transfers between devices: 147 us -> none  [the longest x1 53.6 us: body(): gathered = lax.all_gather(normed, 'head', axis=0, tiled=True)]
    pallas_call x0 -> x1, Pallas kernels: none -> 107 us  [body(): pl.pallas_call(kernel, out_shape=jax.ShapeDtypeStruct((2 * C, D), BF16),...]
    reduce_scatter x1 -> x0, waiting for transfers between devices: 54.4 us -> none  [body(): lax.psum_scatter(jnp.dot(flat_out, w_out, preferred_element_type=jnp.floa...]
    dynamic_slice x96 -> x0, local copies, waits for them, and re-layouts: 51.2 us -> none  [body(): lax.scan(chain_step, empty_state, (all_trans, all_state, jnp.arange(all_t...]
    another operation x2 -> x0, loops' own time: 23.5 us -> none  [the longest x1 22.4 us: body(): lax.scan(chain_step, empty_state, (all_trans, all_state, jnp.arange(all_t...]
    convert_element_type x6 -> x0, other arithmetic: 11.4 us -> none  [the longest x1 4.08 us: body(): lax.all_gather(state_end[None].astype(jnp.bfloat16), 'seq', axis=0, tiled...]
  transfers between devices with their start and end apart: 4 -> 0, of which waited for: 4 -> 0; matrix products, arithmetic and copies ran while one was open for 1% -> 0% of each run, Pallas kernels for 0% -> 0%
where the time goes in v1:
time: 109 us
  Pallas kernels  107 us (98%)
  local copies, waits for them, and re-layouts  1.88 us (2%)
    pallas_call x1, Pallas kernels, body(): pl.pallas_call(kernel, out_shape=jax.ShapeDtypeStruct((2 * C, D), BF16),...  107 us

profile of v1, /device:TPU:1, one launch (start us, length us, event | category | flops | bytes accessed | tf_op | source)
XLA Modules:
  0.0 108.9 jit_solution(3428301604078096286)
XLA Ops:
  0.0 107.0 %delta_layer.1 = bf16[128,2048]{1,0:T(8,128)(2,1)} custom-call(bf16[128,2048]{1,0:T(8,128)(2,1)} %tok_ref.1, bf16[3,2048,256]{2,1,0:T(8,128)(2,1)} %bitcast.3, bf16[2,2048]{1,0:T(2,128)(2,1)} %bitcast.5, f32[2]{0:T(128)} %bias_ref.1, bf16[4,4,16,2048]{3,2,1,0:T(8,128)(2,1)} %bitcast.4), custom_call_target="tpu_custom_call" | custom-call | tf_op jit(solution)/shard_map/delta_layer/pallas_call | solution.py:450
  107.0 1.9 %copy.7 = bf16[128,2048]{1,0:T(8,128)(2,1)} copy(bf16[128,2048]{1,0:T(8,128)(2,1)} %delta_layer.1) | data formatting | bytes 1048576

commit v2 on v1

v2 whole, which is shorter than its diff:
```python
import jax
import jax.numpy as jnp
from jax import lax
from jax.experimental import pallas as pl
from jax.experimental.pallas import tpu as pltpu
from jax.sharding import PartitionSpec as P

F32 = jnp.float32
BF16 = jnp.bfloat16
MESH = pl.DeviceIdType.MESH
EPS = 1e-6
NZ = 8
NX = 4
NY = 4
NC = 2
C = 64
DK = 128
D = 2048

NN = (((1,), (0,)), ((), ()))
NT = (((1,), (1,)), ((), ()))
TN = (((0,), (0,)), ((), ()))


def halves(a):
    hi = a.astype(BF16)
    lo = (a - hi.astype(F32)).astype(BF16)
    return hi, lo


def dot3(a, b, dims=NN):
    ca = dims[0][0][0]
    cb = dims[0][1][0]
    ah, al = halves(a)
    bh, bl = halves(b)
    return lax.dot_general(
        jnp.concatenate([ah, al, ah], ca),
        jnp.concatenate([bh, bh, bl], cb),
        dims,
        preferred_element_type=F32,
    )


def dot1(a, b, dims=NN):
    return lax.dot_general(
        a.astype(BF16), b.astype(BF16), dims, preferred_element_type=F32
    )


def compose(first, second):
    return first + dot3(first, second[:DK]) + second


def kernel(
    tok_ref,
    w3_hbm,
    wb_ref,
    bias_ref,
    wo_hbm,
    out_ref,
    g,
    w3,
    wbt,
    wo,
    qe,
    mu,
    db,
    ct,
    ends,
    tot,
    lv,
    xs,
    xr,
    ys,
    yr,
    eb,
    es,
    sf,
    osend,
    fbuf,
    acc,
    lsem,
    agr_s,
    agr_r,
    agl_s,
    agl_r,
    wzr_s,
    wzr_r,
    wzl_s,
    wzl_r,
    w1_s,
    w1_r,
    w2_s,
    w2_r,
    wc_s,
    wc_r,
    sc_s,
    sc_r,
    a2_s,
    a2_r,
):
    s = lax.axis_index("seq")
    z = lax.axis_index("head")
    c = lax.rem(s, NC)
    x = lax.rem(s // NC, NX)
    y = s // (NC * NX)

    def at_z(d):
        return (s, lax.rem(z + d, NZ))

    def at_x(d):
        return ((y * NX + lax.rem(x + d, NX)) * NC + c, z)

    def at_y(d):
        return ((lax.rem(y + d, NY) * NX + x) * NC + c, z)

    partner = ((y * NX + x) * NC + (1 - c), z)

    peers = [at_z(1), at_z(NZ - 1)]
    peers += [at_x(d) for d in range(1, NX)]
    peers += [at_y(d) for d in range(1, NY)]
    peers += [partner]
    barrier = pltpu.get_barrier_semaphore()
    for p in peers:
        pl.semaphore_signal(barrier, inc=1, device_id=p, device_id_type=MESH)

    cp_w3 = pltpu.make_async_copy(w3_hbm, w3, lsem.at[0])
    cp_w3.start()
    cp_wo = [
        pltpu.make_async_copy(
            wo_hbm.at[:, :, :, pl.ds(q * 1024, 1024)], wo.at[q, z], lsem.at[1 + q]
        )
        for q in range(NC)
    ]
    for cp in cp_wo:
        cp.start()

    for j in range(2):
        t = tok_ref[j * C : (j + 1) * C, :].astype(F32)
        ms = jnp.mean(t * t, -1, keepdims=True)
        g[z, j] = (t * lax.rsqrt(ms + EPS)).astype(BF16)

    def remote(src, dst, ssem, rsem, dev):
        return pltpu.make_async_remote_copy(
            src_ref=src, dst_ref=dst, send_sem=ssem, recv_sem=rsem,
            device_id=dev, device_id_type=MESH,
        )

    def right(i):
        o = lax.rem(z + NZ - i // 2, NZ)
        ref = g.at[o, lax.rem(i, 2)]
        return remote(ref, ref, agr_s.at[i], agr_r.at[i], at_z(1))

    def left(i):
        o = lax.rem(z + i // 2, NZ)
        ref = g.at[o, jnp.where(i == 6, 1, lax.rem(i, 2))]
        return remote(ref, ref, agl_s.at[i], agl_r.at[i], at_z(NZ - 1))

    def wslice(way, k):
        return lax.rem(z + NZ - 1 - k, NZ) if way == 0 else lax.rem(z + 1 + k, NZ)

    def wzr(k):
        ref = wo.at[c, lax.rem(z + NZ - k, NZ), y, x]
        return remote(ref, ref, wzr_s.at[k], wzr_r.at[k], at_z(1))

    def wzl(k):
        ref = wo.at[c, lax.rem(z + k, NZ), y, x]
        return remote(ref, ref, wzl_s.at[k], wzl_r.at[k], at_z(NZ - 1))

    def w1(way, k, d):
        ref = wo.at[c, wslice(way, k), y, x]
        n = way * 12 + k * 3 + d - 1
        dev = at_x(d) if way == 0 else at_y(d)
        return remote(ref, ref, w1_s.at[n], w1_r.at[n], dev)

    def w2(way, k, d):
        o = wslice(way, k)
        ref = wo.at[c, o, y] if way == 0 else wo.at[c, o, :, x]
        n = way * 12 + k * 3 + d - 1
        dev = at_y(d) if way == 0 else at_x(d)
        return remote(ref, ref, w2_s.at[n], w2_r.at[n], dev)

    def wcore(way, k):
        ref = wo.at[c, wslice(way, k)]
        n = way * 4 + k
        return remote(ref, ref, wc_s.at[n], wc_r.at[n], partner)

    ways = (0, 1)

    def start_w1(k, some=ways):
        for way in some:
            for d in range(1, NX):
                w1(way, k, d).start()

    def next_w2(k, some=ways):
        for way in some:
            for d in range(1, NX):
                w1(way, k, d).wait_recv()
            for d in range(1, NX):
                w2(way, k, d).start()

    def next_core(k, some=ways):
        for way in some:
            for d in range(1, NX):
                w2(way, k, d).wait_recv()
            wcore(way, k).start()

    for h in range(2):
        row = jnp.broadcast_to(wb_ref[h : h + 1, :].astype(F32), (DK, D))
        wbt[:, h * DK : (h + 1) * DK] = row.T.astype(BF16)
    cp_w3.wait()

    ri = lax.broadcasted_iota(jnp.int32, (DK, DK), 0)
    ci = lax.broadcasted_iota(jnp.int32, (DK, DK), 1)
    same = (ri // C) == (ci // C)
    strict = same & (ri > ci)
    lower = same & (ri >= ci)
    eye = jnp.where(ri == ci, 1.0, 0.0).astype(F32)

    tile8 = (ri // 8) == (ci // 8)

    def unit(v):
        return v * lax.rsqrt(jnp.sum(v * v, -1, keepdims=True) + EPS)

    def silu(v):
        return v / (1.0 + jnp.exp(-v))

    def joint(pieces):
        rows = jnp.concatenate([g[o, j] for o, j in pieces], 0)
        proj = [
            jnp.dot(rows, w3[p], preferred_element_type=F32) for p in range(3)
        ]
        pre = jnp.dot(rows, wbt[...], preferred_element_type=F32)
        qs = silu(proj[0])
        ks = silu(proj[1])
        vs = silu(proj[2])
        qh = [unit(qs[:, h * DK : (h + 1) * DK]) for h in range(2)]
        kh = [unit(ks[:, h * DK : (h + 1) * DK]) for h in range(2)]
        vh = [vs[:, h * DK : (h + 1) * DK] for h in range(2)]
        bh = [
            1.0 / (1.0 + jnp.exp(-(pre[:, h * DK : (h + 1) * DK] + bias_ref[h])))
            for h in range(2)
        ]
        def both(f, *lists):
            return [f(*args) for args in zip(*lists)]

        def stack(v):
            return [
                jnp.concatenate([v[0][a * C : (a + 1) * C], v[1][a * C : (a + 1) * C]], 0)
                for a in range(2)
            ]

        q, k, v, b = stack(qh), stack(kh), stack(vh), stack(bh)
        gram = both(lambda m: dot3(m, m, NT), k)
        low = both(lambda m, n: jnp.where(strict, m * n, 0.0), gram, b)
        near = both(lambda m: jnp.where(tile8, m, 0.0), low)
        off = both(lambda m: jnp.where(tile8, 0.0, m), low)
        rhs = both(lambda bb, kk, vv: jnp.concatenate([bb * kk, bb * vv], 1), b, k, v)
        near2 = both(dot3, near, near)
        part = both(lambda m, m2: eye - m + dot3(eye - m, m2), near, near2)
        near4 = both(dot3, near2, near2)
        masked = both(lambda m, n: jnp.where(lower, dot1(m, n, NT), 0.0), q, k)
        inv8 = both(lambda m, m4: m + dot3(m, m4), part, near4)
        step1 = both(dot3, inv8, off)
        wu = both(dot3, inv8, rhs)
        step2 = both(dot3, step1, step1)
        wu = both(lambda m, r: r - dot3(m, r), step1, wu)
        step4 = both(dot3, step2, step2)
        wu = both(lambda m, r: r + dot3(m, r), step2, wu)
        wu = both(lambda m, r: r + dot3(m, r), step4, wu)
        mwu = both(dot1, masked, wu)
        pairs = []
        for a in range(2):
            for h in range(2):
                hp = slice(h * C, (h + 1) * C)
                pairs.append(dot3(wu[a][hp], k[a][hp], TN))
        for a, (o, j) in enumerate(pieces):
            blk = 2 * o + j
            for h in range(2):
                hp = slice(h * C, (h + 1) * C)
                pair = pairs[2 * a + h]
                qe[h, blk] = q[a][hp] - mwu[a][hp, :DK]
                mu[h, blk] = mwu[a][hp, DK:]
                db[h, blk, :DK] = -pair[:DK]
                db[h, blk, DK:] = pair[DK:]

    last = lax.rem(z + NZ // 2, NZ)
    zero = jnp.zeros((2 * DK, DK), F32)

    def close_chunk(o):
        for h in range(2):
            d0 = db[h, 2 * o]
            q = qe[h, 2 * o + 1]
            both = dot1(q, d0, NT)
            qe[h, 2 * o + 1] = q + both[:, :DK]
            mu[h, 2 * o + 1] = mu[h, 2 * o + 1] + both[:, DK:]
            ct[h, o] = compose(d0, db[h, 2 * o + 1])

    def run_chain(o, carry):
        nxt = []
        for h in range(2):
            here = ct[h, o]
            ct[h, o] = carry[h]
            nxt.append(compose(carry[h], here))
        return tuple(nxt)

    def work(oa, ja, ob, jb, closing):
        joint([(oa, ja), (ob, jb)])

        def close(n, carry):
            close_chunk(jnp.where(n == 0, oa, ob))
            return carry

        lax.fori_loop(0, closing, close, 0)

    work(z, 0, z, 1, 1)

    for cp in cp_wo:
        cp.wait()
    pl.semaphore_wait(barrier, len(peers))
    for i in range(2):
        right(jnp.int32(i)).start()
        left(jnp.int32(i)).start()
        if i == 0:
            wzr(0).start()
            wzl(0).start()

    def step(t, carry):
        i = t - 1
        mid = t <= 6
        even = lax.rem(t, 2) == 0

        @pl.when(t == 7)
        def _():
            for n, (lo, hi) in enumerate(((0, last), (last + 1, NZ))):
                got = lax.fori_loop(lo, hi, run_chain, (zero, zero))
                for h in range(2):
                    ends[n, h] = got[h]

        def receive():
            @pl.when(even)
            def _():
                k = t // 2 - 1
                wzr(k).wait_recv()
                wzr(k + 1).start()
                wzl(k).wait_recv()

                @pl.when(k <= 1)
                def _():
                    wzl(k + 1).start()

            right(i).wait_recv()

            @pl.when(i <= 4)
            def _():
                right(i + 2).start()

            left(i).wait_recv()

            @pl.when(i <= 3)
            def _():
                left(i + 2).start()

            @pl.when(i == 5)
            def _():
                left(i + 1).start()

            @pl.when(even)
            def _():
                k = t // 2 - 1
                start_w1(k)

                @pl.when(k >= 1)
                def _():
                    next_core(k - 1)

            @pl.when(jnp.logical_and(t >= 3, jnp.logical_not(even)))
            def _():
                next_w2((t - 3) // 2)

            @pl.when(t == 7)
            def _():
                wzr(3).wait_recv()
                start_w1(3, (0,))

        receive()
        hop = (i + 2) // 2
        ja = jnp.where(mid, lax.rem(i, 2), 0)
        jb = jnp.where(mid, lax.rem(i, 2), 1)
        oa = lax.rem(z + NZ - hop, NZ)
        ob = lax.rem(z + hop, NZ)
        work(oa, ja, ob, jb, jnp.where(mid, jnp.where(even, 2, 0), 1))
        return carry

    lax.fori_loop(1, 8, step, 0)

    next_w2(3, (0,))
    for h in range(2):
        pre = ends[0, h]
        upto = compose(pre, ct[h, last])
        ct[h, last] = pre
        tot[h] = compose(upto, ends[1, h])
        ends[0, h] = upto

    def core_swap():
        return remote(tot.at[1 - c], lv.at[c], sc_s.at[0], sc_r.at[0], partner)

    core_swap().start()
    lv[c] = tot[c]

    def fold_queries(first, final):
        def one(o, carry):
            after = jnp.broadcast_to((o > last).astype(jnp.int32), (2 * DK, DK)) > 0
            for h in range(2):
                m = compose(jnp.where(after, ends[0, h], 0.0), ct[h, o])
                q = jnp.concatenate([qe[h, 2 * o], qe[h, 2 * o + 1]], 0)
                both = dot1(q, m, NT)
                new = q + both[:, :DK]
                qe[h, 2 * o] = new[:C]
                qe[h, 2 * o + 1] = new[C:]
                mu[h, 2 * o] = mu[h, 2 * o] + both[:C, DK:]
                mu[h, 2 * o + 1] = mu[h, 2 * o + 1] + both[C:, DK:]
            return carry

        lax.fori_loop(first, final, one, 0)

    core_swap().wait_recv()

    group = compose(lv[0], lv[1])
    before = jnp.zeros((2 * DK, DK), F32)
    xp = jnp.where(lax.rem(x, 2) == 0, 1, NX - 1)
    yp = jnp.where(lax.rem(y, 2) == 0, 1, NY - 1)
    xq = lax.rem(2 * NX - 1 - 2 * x, NX)
    yq = lax.rem(2 * NY - 1 - 2 * y, NY)
    levels = [
        (at_x(xp), lax.rem(x, 2) == 0),
        (at_x(xq), x < 2),
        (at_y(yp), lax.rem(y, 2) == 0),
        (at_y(yq), y < 2),
    ]
    sends = []
    for n, (dev, is_low) in enumerate(levels[:3]):
        xs[n] = group.astype(BF16)
        cp = remote(xs.at[n], xr.at[n], sc_s.at[n + 1], sc_r.at[n + 1], dev)
        cp.start()
        sends.append(cp)
        fold_queries(2 * n, 2 * n + 2)
        cp.wait_recv()
        other = xr[n].astype(F32)
        low = jnp.broadcast_to(is_low.astype(jnp.int32), (2 * DK, DK)) > 0
        group = compose(jnp.where(low, group, other), jnp.where(low, other, group))
        before = jnp.where(low, before, compose(other, before))
        if n == 0:
            next_core(2)
        if n == 1:
            next_core(3, (0,))

    ys[...] = group[DK:].astype(BF16)
    far, _ = levels[3]
    for q in range(NC):
        dev = (far[0] - c + q, z)
        cp = remote(ys, yr.at[c], sc_s.at[4 + q], sc_r.at[4 + c], dev)
        cp.start()
        sends.append(cp)

    def got_y(h):
        return remote(ys, yr.at[h], sc_s.at[4 + h], sc_r.at[4 + h], partner)

    before1 = compose(before, lv[0])
    zero_core = jnp.broadcast_to(c, (2 * DK, DK)) == 0
    es[...] = jnp.where(zero_core, before1, before)
    give = remote(es, eb.at[c], sc_s.at[6], sc_r.at[6], partner)
    give.start()
    eb[c] = jnp.where(zero_core, before, before1)
    fold_queries(6, 8)
    give.wait_recv()
    high = jnp.broadcast_to((y >= 2).astype(jnp.int32), (DK, DK)) > 0
    sin = []
    for h in range(2):
        got_y(h).wait_recv()
        base = jnp.where(high, yr[h].astype(F32), 0.0)
        sin.append(base + dot3(base, eb[h, :DK]) + eb[h, DK:])
    for h in range(2):
        sf[h] = sin[h]

    def a2a(d, o):
        return remote(osend.at[o], fbuf.at[z], a2_s.at[d - 1], a2_r.at[d - 1], (s, o))

    def emit(i, carry):
        d = jnp.where(lax.rem(i, 2) == 1, 4 - (i + 1) // 2, 4 + i // 2)
        o = lax.rem(z + d, NZ)
        cols = []
        for h in range(2):
            q = jnp.concatenate([qe[h, 2 * o], qe[h, 2 * o + 1]], 0)
            m = jnp.concatenate([mu[h, 2 * o], mu[h, 2 * o + 1]], 0)
            full = m + dot1(q, sf[h], NT)
            ms = jnp.mean(full * full, -1, keepdims=True)
            cols.append((full * lax.rsqrt(ms + EPS)).astype(BF16))
        rows = jnp.concatenate(cols, 1)

        @pl.when(i < 7)
        def _():
            osend[o] = rows
            a2a(d, o).start()

        @pl.when(i == 7)
        def _():
            fbuf[z] = rows

        return carry

    lax.fori_loop(0, NZ, emit, 0)

    for k in range(4):
        wcore(0, k).wait_recv()
        if k < 3:
            wcore(1, k).wait_recv()

    def finish(i, carry):
        n = i - 1
        d = jnp.where(lax.rem(n, 2) == 1, 4 - (n + 1) // 2, 4 + n // 2)
        d = jnp.where(i == 0, 0, d)
        src = lax.rem(z + NZ - d, NZ)

        @pl.when(i >= 1)
        def _():
            remote(
                osend.at[src], fbuf.at[src], a2_s.at[d - 1], a2_r.at[d - 1], (s, src)
            ).wait_recv()

        rows = fbuf[src]
        for half in range(2):
            w = wo[half, src].reshape(2 * DK, 1024)
            term = jnp.dot(rows, w, preferred_element_type=F32)
            cols = slice(half * 1024, (half + 1) * 1024)

            @pl.when(i == 0)
            def _():
                acc[:, cols] = term

            @pl.when(i >= 1)
            def _():
                acc[:, cols] = acc[:, cols] + term

        return carry

    lax.fori_loop(0, NZ, finish, 0)
    out_ref[...] = acc[...].astype(BF16)

    for i in range(7):
        right(jnp.int32(i)).wait_send()
        left(jnp.int32(i)).wait_send()
    for d in range(1, NZ):
        a2a(d, lax.rem(z + d, NZ)).wait_send()
    for k in range(4):
        wzr(k).wait_send()
        for way in ways[: 2 if k < 3 else 1]:
            wcore(way, k).wait_send()
            for d in range(1, NX):
                w1(way, k, d).wait_send()
                w2(way, k, d).wait_send()
        if k < 3:
            wzl(k).wait_send()
    core_swap().wait_send()
    for cp in sends:
        cp.wait_send()
    give.wait_send()


def body(tokens, w_qkv, w_beta, beta_bias, w_out):
    w3 = jnp.transpose(w_qkv, (1, 0, 2))
    wb = jnp.transpose(w_beta, (1, 0))
    wo = w_out.reshape(NY, NX, 16, D)
    vmem = pl.BlockSpec(memory_space=pltpu.VMEM)
    hbm = pl.BlockSpec(memory_space=pl.ANY)
    smem = pl.BlockSpec(memory_space=pltpu.SMEM)
    dma = pltpu.SemaphoreType.DMA
    return pl.pallas_call(
        kernel,
        out_shape=jax.ShapeDtypeStruct((2 * C, D), BF16),
        in_specs=[vmem, hbm, vmem, smem, hbm],
        out_specs=vmem,
        scratch_shapes=[
            pltpu.VMEM((NZ, 2, C, D), BF16),
            pltpu.VMEM((3, D, 2 * DK), BF16),
            pltpu.VMEM((D, 2 * DK), BF16),
            pltpu.VMEM((2, NZ, NY, NX, 16, 1024), BF16),
            pltpu.VMEM((2, 16, C, DK), F32),
            pltpu.VMEM((2, 16, C, DK), F32),
            pltpu.VMEM((2, 16, 2 * DK, DK), F32),
            pltpu.VMEM((2, NZ, 2 * DK, DK), F32),
            pltpu.VMEM((2, 2, 2 * DK, DK), F32),
            pltpu.VMEM((2, 2 * DK, DK), F32),
            pltpu.VMEM((2, 2 * DK, DK), F32),
            pltpu.VMEM((3, 2 * DK, DK), BF16),
            pltpu.VMEM((3, 2 * DK, DK), BF16),
            pltpu.VMEM((DK, DK), BF16),
            pltpu.VMEM((2, DK, DK), BF16),
            pltpu.VMEM((2, 2 * DK, DK), F32),
            pltpu.VMEM((2 * DK, DK), F32),
            pltpu.VMEM((2, DK, DK), F32),
            pltpu.VMEM((NZ, 2 * C, 2 * DK), BF16),
            pltpu.VMEM((NZ, 2 * C, 2 * DK), BF16),
            pltpu.VMEM((2 * C, D), F32),
            dma((3,)),
            dma((7,)),
            dma((7,)),
            dma((7,)),
            dma((7,)),
            dma((4,)),
            dma((4,)),
            dma((3,)),
            dma((3,)),
            dma((21,)),
            dma((21,)),
            dma((21,)),
            dma((21,)),
            dma((7,)),
            dma((7,)),
            dma((7,)),
            dma((7,)),
            dma((7,)),
            dma((7,)),
        ],
        compiler_params=pltpu.CompilerParams(
            collective_id=0, has_side_effects=True, vmem_limit_bytes=60 * 1024 * 1024
        ),
        name="delta_layer",
    )(tokens, w3, wb, beta_bias, wo)


def solution(mesh):
    return jax.shard_map(
        body,
        mesh=mesh,
        in_specs=(
            P(("seq", "head"), None),
            P(None, None, "head"),
            P(None, "head"),
            P("head"),
            P("head", None),
        ),
        out_specs=P(("seq", "head"), None),
        check_vma=False,
    )
```

time: 109 us -> 102 us (0.936)
  Pallas kernels: 107 us -> 99.7 us
    pallas_call x1, Pallas kernels: 107 us -> 99.7 us  [body(): pl.pallas_call(kernel, out_shape=jax.ShapeDtypeStruct((2 * C, D), BF16),...]
where the time goes in v2:
time: 102 us
  Pallas kernels  99.7 us (98%)
  local copies, waits for them, and re-layouts  1.88 us (2%)
    pallas_call x1, Pallas kernels, body(): pl.pallas_call(kernel, out_shape=jax.ShapeDtypeStruct((2 * C, D), BF16),...  99.7 us

profile of v2, /device:TPU:1, one launch (start us, length us, event | category | flops | bytes accessed | tf_op | source)
XLA Modules:
  0.0 101.6 jit_solution(5411162235663013268)
XLA Ops:
  0.0 99.7 %delta_layer.1 = bf16[128,2048]{1,0:T(8,128)(2,1)} custom-call(bf16[128,2048]{1,0:T(8,128)(2,1)} %tok_ref.1, bf16[3,2048,256]{2,1,0:T(8,128)(2,1)} %bitcast.3, bf16[2,2048]{1,0:T(2,128)(2,1)} %bitcast.5, f32[2]{0:T(128)} %bias_ref.1, bf16[4,4,16,2048]{3,2,1,0:T(8,128)(2,1)} %bitcast.4), custom_call_target="tpu_custom_call" | custom-call | tf_op jit(solution)/shard_map/delta_layer/pallas_call | solution.py:578
  99.7 1.9 %copy.7 = bf16[128,2048]{1,0:T(8,128)(2,1)} copy(bf16[128,2048]{1,0:T(8,128)(2,1)} %delta_layer.1) | data formatting | bytes 1048576

commit v3 on v2

--- a/solution.py
+++ b/solution.py
@@ -71,6 +71,7 @@
     lv,
     xs,
     xr,
+    xg,
     ys,
     yr,
     eb,
@@ -205,9 +206,18 @@
                 w2(way, k, d).wait_recv()
             wcore(way, k).start()
 
-    for h in range(2):
-        row = jnp.broadcast_to(wb_ref[h : h + 1, :].astype(F32), (DK, D))
-        wbt[:, h * DK : (h + 1) * DK] = row.T.astype(BF16)
+    wbt[...] = jnp.concatenate(
+        [wb_ref[...].astype(F32), jnp.zeros((DK - 2, D), F32)], 0
+    ).T.astype(BF16)
+
+    for cp in cp_wo:
+        cp.wait()
+    pl.semaphore_wait(barrier, len(peers))
+    wzr(0).start()
+    wzl(0).start()
+    for i in range(2):
+        right(jnp.int32(i)).start()
+        left(jnp.int32(i)).start()
     cp_w3.wait()
 
     ri = lax.broadcasted_iota(jnp.int32, (DK, DK), 0)
@@ -238,7 +248,7 @@
         kh = [unit(ks[:, h * DK : (h + 1) * DK]) for h in range(2)]
         vh = [vs[:, h * DK : (h + 1) * DK] for h in range(2)]
         bh = [
-            1.0 / (1.0 + jnp.exp(-(pre[:, h * DK : (h + 1) * DK] + bias_ref[h])))
+            1.0 / (1.0 + jnp.exp(-(jnp.broadcast_to(pre[:, h : h + 1], (DK, DK)) + bias_ref[h])))
             for h in range(2)
         ]
         def both(f, *lists):
@@ -287,14 +297,16 @@
     last = lax.rem(z + NZ // 2, NZ)
     zero = jnp.zeros((2 * DK, DK), F32)
 
+    def fold_second(o, h):
+        q = qe[h, 2 * o + 1]
+        both = dot1(q, db[h, 2 * o], NT)
+        qe[h, 2 * o + 1] = q + both[:, :DK]
+        mu[h, 2 * o + 1] = mu[h, 2 * o + 1] + both[:, DK:]
+
     def close_chunk(o):
         for h in range(2):
-            d0 = db[h, 2 * o]
-            q = qe[h, 2 * o + 1]
-            both = dot1(q, d0, NT)
-            qe[h, 2 * o + 1] = q + both[:, :DK]
-            mu[h, 2 * o + 1] = mu[h, 2 * o + 1] + both[:, DK:]
-            ct[h, o] = compose(d0, db[h, 2 * o + 1])
+            fold_second(o, h)
+            ct[h, o] = compose(db[h, 2 * o], db[h, 2 * o + 1])
 
     def run_chain(o, carry):
         nxt = []
@@ -315,16 +327,6 @@
 
     work(z, 0, z, 1, 1)
 
-    for cp in cp_wo:
-        cp.wait()
-    pl.semaphore_wait(barrier, len(peers))
-    for i in range(2):
-        right(jnp.int32(i)).start()
-        left(jnp.int32(i)).start()
-        if i == 0:
-            wzr(0).start()
-            wzl(0).start()
-
     def step(t, carry):
         i = t - 1
         mid = t <= 6
@@ -332,75 +334,72 @@
 
         @pl.when(t == 7)
         def _():
+            wzr(3).wait_recv()
+            start_w1(3, (0,))
             for n, (lo, hi) in enumerate(((0, last), (last + 1, NZ))):
                 got = lax.fori_loop(lo, hi, run_chain, (zero, zero))
                 for h in range(2):
                     ends[n, h] = got[h]
 
-        def receive():
-            @pl.when(even)
+        early = jnp.logical_and(jnp.logical_not(even), mid)
+
+        @pl.when(early)
+        def _():
+            k = i // 2
+            wzr(k).wait_recv()
+            wzr(k + 1).start()
+            wzl(k).wait_recv()
+
+            @pl.when(k <= 1)
             def _():
-                k = t // 2 - 1
-                wzr(k).wait_recv()
-                wzr(k + 1).start()
-                wzl(k).wait_recv()
-
-                @pl.when(k <= 1)
-                def _():
-                    wzl(k + 1).start()
-
-            right(i).wait_recv()
-
-            @pl.when(i <= 4)
+                wzl(k + 1).start()
+
+        right(i).wait_recv()
+
+        @pl.when(i <= 4)
+        def _():
+            right(i + 2).start()
+
+        left(i).wait_recv()
+
+        @pl.when(i <= 3)
+        def _():
+            left(i + 2).start()
+
+        @pl.when(i == 5)
+        def _():
+            left(i + 1).start()
+
+        @pl.when(early)
+        def _():
+            start_w1(i // 2)
+
+        @pl.when(even)
+        def _():
+            next_w2(t // 2 - 1)
+
+            @pl.when(t >= 4)
             def _():
-                right(i + 2).start()
-
-            left(i).wait_recv()
-
-            @pl.when(i <= 3)
-            def _():
-                left(i + 2).start()
-
-            @pl.when(i == 5)
-            def _():
-                left(i + 1).start()
-
-            @pl.when(even)
-            def _():
-                k = t // 2 - 1
-                start_w1(k)
-
-                @pl.when(k >= 1)
-                def _():
-                    next_core(k - 1)
-
-            @pl.when(jnp.logical_and(t >= 3, jnp.logical_not(even)))
-            def _():
-                next_w2((t - 3) // 2)
-
-            @pl.when(t == 7)
-            def _():
-                wzr(3).wait_recv()
-                start_w1(3, (0,))
-
-        receive()
+                next_core(t // 2 - 2)
+
+        @pl.when(t == 7)
+        def _():
+            next_w2(3, (0,))
+
         hop = (i + 2) // 2
         ja = jnp.where(mid, lax.rem(i, 2), 0)
         jb = jnp.where(mid, lax.rem(i, 2), 1)
         oa = lax.rem(z + NZ - hop, NZ)
         ob = lax.rem(z + hop, NZ)
-        work(oa, ja, ob, jb, jnp.where(mid, jnp.where(even, 2, 0), 1))
+        work(oa, ja, ob, jb, jnp.where(jnp.logical_and(mid, even), 2, 0))
         return carry
 
     lax.fori_loop(1, 8, step, 0)
 
-    next_w2(3, (0,))
+    head = [compose(ends[0, h], db[h, 2 * last]) for h in range(2)]
+    rest = [compose(db[h, 2 * last + 1], ends[1, h]) for h in range(2)]
     for h in range(2):
-        pre = ends[0, h]
-        upto = compose(pre, ct[h, last])
-        ct[h, last] = pre
-        tot[h] = compose(upto, ends[1, h])
-        ends[0, h] = upto
+        tot[h] = compose(head[h], rest[h])
 
     def core_swap():
         return remote(tot.at[1 - c], lv.at[c], sc_s.at[0], sc_r.at[0], partner)
@@ -424,39 +423,49 @@
 
         lax.fori_loop(first, final, one, 0)
 
+    for h in range(2):
+        ct[h, last] = ends[0, h]
+        ends[0, h] = compose(head[h], db[h, 2 * last + 1])
+        fold_second(last, h)
     core_swap().wait_recv()
 
     group = compose(lv[0], lv[1])
-    before = jnp.zeros((2 * DK, DK), F32)
-    xp = jnp.where(lax.rem(x, 2) == 0, 1, NX - 1)
-    yp = jnp.where(lax.rem(y, 2) == 0, 1, NY - 1)
-    xq = lax.rem(2 * NX - 1 - 2 * x, NX)
-    yq = lax.rem(2 * NY - 1 - 2 * y, NY)
-    levels = [
-        (at_x(xp), lax.rem(x, 2) == 0),
-        (at_x(xq), x < 2),
-        (at_y(yp), lax.rem(y, 2) == 0),
-        (at_y(yq), y < 2),
-    ]
     sends = []
-    for n, (dev, is_low) in enumerate(levels[:3]):
-        xs[n] = group.astype(BF16)
-        cp = remote(xs.at[n], xr.at[n], sc_s.at[n + 1], sc_r.at[n + 1], dev)
+    xs[0] = group.astype(BF16)
+    for d in range(1, NX):
+        cp = remote(xs.at[0], xg.at[x], sc_s.at[d], sc_r.at[d], at_x(d))
         cp.start()
         sends.append(cp)
-        fold_queries(2 * n, 2 * n + 2)
-        cp.wait_recv()
-        other = xr[n].astype(F32)
-        low = jnp.broadcast_to(is_low.astype(jnp.int32), (2 * DK, DK)) > 0
-        group = compose(jnp.where(low, group, other), jnp.where(low, other, group))
-        before = jnp.where(low, before, compose(other, before))
-        if n == 0:
-            next_core(2)
-        if n == 1:
-            next_core(3, (0,))
+    xg[x] = group.astype(BF16)
+    fold_queries(0, 4)
+    for d in range(1, NX):
+        sends[d - 1].wait_recv()
+    part = [xg[n].astype(F32) for n in range(NX)]
+    p01 = compose(part[0], part[1])
+    p23 = compose(part[2], part[3])
+    p012 = compose(p01, part[2])
+    group = compose(p01, p23)
+    xv = jnp.broadcast_to(x, (2 * DK, DK))
+    before = jnp.where(xv == 1, part[0], 0.0)
+    before = jnp.where(xv == 2, p01, before)
+    before = jnp.where(xv == 3, p012, before)
+
+    yp = jnp.where(lax.rem(y, 2) == 0, 1, NY - 1)
+    yq = lax.rem(2 * NY - 1 - 2 * y, NY)
+    xs[1] = group.astype(BF16)
+    cp = remote(xs.at[1], xr, sc_s.at[7], sc_r.at[7], at_y(yp))
+    cp.start()
+    sends.append(cp)
+    next_core(2)
+    fold_queries(4, 6)
+    cp.wait_recv()
+    other = xr[...].astype(F32)
+    low = jnp.broadcast_to(lax.rem(y, 2), (2 * DK, DK)) == 0
+    group = compose(jnp.where(low, group, other), jnp.where(low, other, group))
+    before = jnp.where(low, before, compose(other, before))
 
     ys[...] = group[DK:].astype(BF16)
-    far, _ = levels[3]
+    far = at_y(yq)
     for q in range(NC):
         dev = (far[0] - c + q, z)
         cp = remote(ys, yr.at[c], sc_s.at[4 + q], sc_r.at[4 + c], dev)
@@ -472,6 +481,7 @@
     give = remote(es, eb.at[c], sc_s.at[6], sc_r.at[6], partner)
     give.start()
     eb[c] = jnp.where(zero_core, before, before1)
+    next_core(3, (0,))
     fold_queries(6, 8)
     give.wait_recv()
     high = jnp.broadcast_to((y >= 2).astype(jnp.int32), (DK, DK)) > 0
@@ -583,7 +593,7 @@
         scratch_shapes=[
             pltpu.VMEM((NZ, 2, C, D), BF16),
             pltpu.VMEM((3, D, 2 * DK), BF16),
-            pltpu.VMEM((D, 2 * DK), BF16),
+            pltpu.VMEM((D, DK), BF16),
             pltpu.VMEM((2, NZ, NY, NX, 16, 1024), BF16),
             pltpu.VMEM((2, 16, C, DK), F32),
             pltpu.VMEM((2, 16, C, DK), F32),
@@ -592,8 +602,9 @@
             pltpu.VMEM((2, 2, 2 * DK, DK), F32),
             pltpu.VMEM((2, 2 * DK, DK), F32),
             pltpu.VMEM((2, 2 * DK, DK), F32),
-            pltpu.VMEM((3, 2 * DK, DK), BF16),
-            pltpu.VMEM((3, 2 * DK, DK), BF16),
+            pltpu.VMEM((2, 2 * DK, DK), BF16),
+            pltpu.VMEM((2 * DK, DK), BF16),
+            pltpu.VMEM((NX, 2 * DK, DK), BF16),
             pltpu.VMEM((DK, DK), BF16),
             pltpu.VMEM((2, DK, DK), BF16),
             pltpu.VMEM((2, 2 * DK, DK), F32),
@@ -617,8 +628,8 @@
             dma((21,)),
             dma((7,)),
             dma((7,)),
-            dma((7,)),
-            dma((7,)),
+            dma((8,)),
+            dma((8,)),
             dma((7,)),
             dma((7,)),
         ],

time: 102 us -> 94.2 us (0.924)
  Pallas kernels: 99.7 us -> 92.2 us
    pallas_call x1, Pallas kernels: 99.7 us -> 92.2 us  [body(): pl.pallas_call(kernel, out_shape=jax.ShapeDtypeStruct((2 * C, D), BF16),...]
where the time goes in v3:
time: 94.2 us; the launch traced here: 94.1 us
  Pallas kernels  92.2 us (98%)
  local copies, waits for them, and re-layouts  1.88 us (2%)
    pallas_call x1, Pallas kernels, body(): pl.pallas_call(kernel, out_shape=jax.ShapeDtypeStruct((2 * C, D), BF16),...  92.2 us

profile of v3, /device:TPU:1, one launch (start us, length us, event | category | flops | bytes accessed | tf_op | source)
XLA Modules:
  0.0 94.1 jit_solution(17563577690781248577)
XLA Ops:
  0.0 92.2 %delta_layer.1 = bf16[128,2048]{1,0:T(8,128)(2,1)} custom-call(bf16[128,2048]{1,0:T(8,128)(2,1)} %tok_ref.1, bf16[3,2048,256]{2,1,0:T(8,128)(2,1)} %bitcast.3, bf16[2,2048]{1,0:T(2,128)(2,1)} %bitcast.5, f32[2]{0:T(128)} %bias_ref.1, bf16[4,4,16,2048]{3,2,1,0:T(8,128)(2,1)} %bitcast.4), custom_call_target="tpu_custom_call" | custom-call | tf_op jit(solution)/shard_map/delta_layer/pallas_call | solution.py:588
  92.2 1.9 %copy.7 = bf16[128,2048]{1,0:T(8,128)(2,1)} copy(bf16[128,2048]{1,0:T(8,128)(2,1)} %delta_layer.1) | data formatting | bytes 1048576

commit v4 on v3

--- a/solution.py
+++ b/solution.py
@@ -80,6 +80,7 @@
     osend,
     fbuf,
     acc,
+    hello,
     lsem,
     agr_s,
     agr_r,
@@ -118,9 +119,7 @@
     partner = ((y * NX + x) * NC + (1 - c), z)
 
     peers = [at_z(1), at_z(NZ - 1)]
-    peers += [at_x(d) for d in range(1, NX)]
-    peers += [at_y(d) for d in range(1, NY)]
-    peers += [partner]
+    peers += [at_x(1), at_x(NX - 1), at_y(1), at_y(NY - 1), partner]
     barrier = pltpu.get_barrier_semaphore()
     for p in peers:
         pl.semaphore_signal(barrier, inc=1, device_id=p, device_id_type=MESH)
@@ -206,18 +205,21 @@
                 w2(way, k, d).wait_recv()
             wcore(way, k).start()
 
+    pl.semaphore_wait(barrier, len(peers))
+    first = jnp.int32(0)
+    right(first).start()
+    left(first).start()
+    for cp in cp_wo:
+        cp.wait()
+    wzr(0).start()
+    wzl(0).start()
+    right(first + 1).start()
+    left(first + 1).start()
+    for dev in (at_x(NX - 1), at_y(NY - 1)):
+        pl.semaphore_signal(hello, inc=1, device_id=dev, device_id_type=MESH)
     wbt[...] = jnp.concatenate(
         [wb_ref[...].astype(F32), jnp.zeros((DK - 2, D), F32)], 0
     ).T.astype(BF16)
-
-    for cp in cp_wo:
-        cp.wait()
-    pl.semaphore_wait(barrier, len(peers))
-    wzr(0).start()
-    wzl(0).start()
-    for i in range(2):
-        right(jnp.int32(i)).start()
-        left(jnp.int32(i)).start()
     cp_w3.wait()
 
     ri = lax.broadcasted_iota(jnp.int32, (DK, DK), 0)
@@ -326,6 +328,7 @@
         lax.fori_loop(0, closing, close, 0)
 
     work(z, 0, z, 1, 1)
+    pl.semaphore_wait(hello, 2)
 
     def step(t, carry):
         i = t - 1
@@ -613,6 +616,7 @@
             pltpu.VMEM((NZ, 2 * C, 2 * DK), BF16),
             pltpu.VMEM((NZ, 2 * C, 2 * DK), BF16),
             pltpu.VMEM((2 * C, D), F32),
+            pltpu.SemaphoreType.REGULAR,
             dma((3,)),
             dma((7,)),
             dma((7,)),

time: 94.2 us -> 93.8 us (level)
  no operation moved by 1% of the time
where the time goes in v4:
time: 93.8 us; the launch traced here: 93.6 us
  Pallas kernels  91.8 us (98%)
  local copies, waits for them, and re-layouts  1.88 us (2%)
    pallas_call x1, Pallas kernels, body(): pl.pallas_call(kernel, out_shape=jax.ShapeDtypeStruct((2 * C, D), BF16),...  91.8 us
    unnamed x1, local copies, waits for them, and re-layouts  1.88 us

profile of v4, /device:TPU:1, one launch (start us, length us, event | category | flops | bytes accessed | tf_op | source)
XLA Modules:
  0.0 93.6 jit_solution(7994882351146358743)
XLA Ops:
  0.0 91.8 %delta_layer.1 = bf16[128,2048]{1,0:T(8,128)(2,1)} custom-call(bf16[128,2048]{1,0:T(8,128)(2,1)} %tok_ref.1, bf16[3,2048,256]{2,1,0:T(8,128)(2,1)} %bitcast.3, bf16[2,2048]{1,0:T(2,128)(2,1)} %bitcast.5, f32[2]{0:T(128)} %bias_ref.1, bf16[4,4,16,2048]{3,2,1,0:T(8,128)(2,1)} %bitcast.4), custom_call_target="tpu_custom_call" | custom-call | tf_op jit(solution)/shard_map/delta_layer/pallas_call | solution.py:591
  91.8 1.9 %copy.7 = bf16[128,2048]{1,0:T(8,128)(2,1)} copy(bf16[128,2048]{1,0:T(8,128)(2,1)} %delta_layer.1) | data formatting | bytes 1048576

commit v5 on v4

--- a/solution.py
+++ b/solution.py
@@ -435,7 +435,7 @@
     group = compose(lv[0], lv[1])
     sends = []
     xs[0] = group.astype(BF16)
-    for d in range(1, NX):
+    for d in (2, 1, 3):
         cp = remote(xs.at[0], xg.at[x], sc_s.at[d], sc_r.at[d], at_x(d))
         cp.start()
         sends.append(cp)

time: 93.8 us -> 93.3 us (level)
  no operation moved by 1% of the time
where the time goes in v5:
time: 93.3 us; the launch traced here: 93.1 us
  Pallas kernels  91.2 us (98%)
  local copies, waits for them, and re-layouts  1.88 us (2%)
    pallas_call x1, Pallas kernels, body(): pl.pallas_call(kernel, out_shape=jax.ShapeDtypeStruct((2 * C, D), BF16),...  91.2 us
    unnamed x1, local copies, waits for them, and re-layouts  1.88 us

profile of v5, /device:TPU:1, one launch (start us, length us, event | category | flops | bytes accessed | tf_op | source)
XLA Modules:
  0.0 93.1 jit_solution(6404987884073029192)
XLA Ops:
  0.0 91.2 %delta_layer.1 = bf16[128,2048]{1,0:T(8,128)(2,1)} custom-call(bf16[128,2048]{1,0:T(8,128)(2,1)} %tok_ref.1, bf16[3,2048,256]{2,1,0:T(8,128)(2,1)} %bitcast.3, bf16[2,2048]{1,0:T(2,128)(2,1)} %bitcast.5, f32[2]{0:T(128)} %bias_ref.1, bf16[4,4,16,2048]{3,2,1,0:T(8,128)(2,1)} %bitcast.4), custom_call_target="tpu_custom_call" | custom-call | tf_op jit(solution)/shard_map/delta_layer/pallas_call | solution.py:591
  91.2 1.9 %copy.7 = bf16[128,2048]{1,0:T(8,128)(2,1)} copy(bf16[128,2048]{1,0:T(8,128)(2,1)} %delta_layer.1) | data formatting | bytes 1048576
